TPU v7x, 32 devices: a whole 2x2x4 slice. The times are simulated.
32 devices in a mesh: section: 2 (over y), dp: 16 (over z, x, core).
Axes of the slice: x: 2, y: 2, z: 4, core: 2. Of those that a mesh axis runs over, the one named last changes fastest.
Arguments:
- inputs: bfloat16 [2, 16, 64, 1024], P(None, 'dp'), may hold values from -6 to 6
- cotangent: bfloat16 [2, 16, 64, 1024], P(None, 'dp'), may hold values from -6 to 6
- live_slots: int32 [2, 16], P(None, 'dp'), may hold values 0 or 1
- norm1_gain: bfloat16 [2, 1024], P('section', 'dp'), may hold values from 0.099609375 to 1.8984375
- norm1_bias: bfloat16 [2, 1024], P('section', 'dp'), may hold values from -4 to 4
- qkv_weight: bfloat16 [2, 1024, 3072], P('section', 'dp')
- qv_bias: bfloat16 [2, 2048], P('section', 'dp'), may hold values from -6 to 6
- out_weight: bfloat16 [2, 1024, 1024], P('section', 'dp'), may hold values from -0.75 to 0.75
- out_bias: bfloat16 [2, 1024], P('section', 'dp'), may hold values from -4 to 4
- norm2_gain: bfloat16 [2, 1024], P('section', 'dp'), may hold values from 0.099609375 to 1.8984375
- norm2_bias: bfloat16 [2, 1024], P('section', 'dp'), may hold values from -4 to 4
- fc1_weight: bfloat16 [2, 1024, 4096], P('section', 'dp'), may hold values from -0.1875 to 0.1875
- fc1_bias: bfloat16 [2, 4096], P('section', 'dp'), may hold values from -6 to 6
- fc2_weight: bfloat16 [2, 4096, 1024], P('section', 'dp'), may hold values from -0.09375 to 0.09375
- fc2_bias: bfloat16 [2, 1024], P('section', 'dp'), may hold values from -4 to 4
Outputs:
- outputs: bfloat16 [2, 2, 16, 64, 1024], P('section', None, 'dp')
- in_grads: float32 [2, 2, 16, 64, 1024], P('section', None, 'dp')
- norm1_gain_grad: float32 [2, 1024], P('section', 'dp')
- norm1_bias_grad: float32 [2, 1024], P('section', 'dp')
- qkv_weight_grad: float32 [2, 1024, 3072], P('section', 'dp')
- qv_bias_grad: float32 [2, 2048], P('section', 'dp')
- out_weight_grad: float32 [2, 1024, 1024], P('section', 'dp')
- out_bias_grad: float32 [2, 1024], P('section', 'dp')
- norm2_gain_grad: float32 [2, 1024], P('section', 'dp')
- norm2_bias_grad: float32 [2, 1024], P('section', 'dp')
- fc1_weight_grad: float32 [2, 1024, 4096], P('section', 'dp')
- fc1_bias_grad: float32 [2, 4096], P('section', 'dp')
- fc2_weight_grad: float32 [2, 4096, 1024], P('section', 'dp')
- fc2_bias_grad: float32 [2, 1024], P('section', 'dp')
All inputs are finite; a program needn't handle non-finite values. No bound on the sum of `live_slots` on one device may be relied on, other than what follows from the above.
Results may differ from a plain program's by a relative error of at most 0.018.
Values may be sent and summed in bfloat16 or wider, within the bound.
A program may use at most 192 MiB of HBM per device.

v0:
```python
import jax
import jax.numpy as jnp
from jax import lax
from jax.sharding import PartitionSpec as P

HEAD_DIM = 64


EPSILON = 1e-06
ROOT_HALF = 0.7071067811865476
INV_ROOT_TWO_PI = 0.3989422804014327


def passed_along(value, axis, steps):
    count = lax.axis_size(axis)
    leading, last = (max(0, -steps), min(count, count - steps))
    return lax.ppermute(value, axis, [(source, source + steps) for source in range(leading, last)])


def norm_parts(stream):
    average = jnp.mean(stream, axis=-1, keepdims=True)
    centred = stream - average
    inv_std = lax.rsqrt(jnp.mean(centred * centred, axis=-1, keepdims=True) + EPSILON)
    return (centred * inv_std, inv_std)


def norm_back(signal, normed, inv_std):
    first_mean = jnp.mean(signal, axis=-1, keepdims=True)
    second_mean = jnp.mean(signal * normed, axis=-1, keepdims=True)
    return inv_std * (signal - first_mean - normed * second_mean)


def gelu_value(pre_act):
    return 0.5 * pre_act * (1.0 + lax.erf(pre_act * ROOT_HALF))


def gelu_slope(pre_act):
    return (
        0.5 * (1.0 + lax.erf(pre_act * ROOT_HALF))
        + pre_act * jnp.exp(-0.5 * pre_act * pre_act) * INV_ROOT_TWO_PI
    )


def matmul(left_rows, weight):
    return jnp.einsum("bsd,de->bse", left_rows, weight, preferred_element_type=jnp.float32)


def transposed_product(left_rows, weight):
    return jnp.einsum("bse,de->bsd", left_rows, weight, preferred_element_type=jnp.float32)


def layer_forward(stream, live_scale, params):
    (
        norm1_gain,
        norm1_bias,
        qkv_weight,
        qv_bias,
        out_weight,
        out_bias,
        norm2_gain,
        norm2_bias,
        fc1_weight,
        fc1_bias,
        fc2_weight,
        fc2_bias,
    ) = params
    images, length, model_width = stream.shape
    heads_shape = (images, length, model_width // HEAD_DIM, HEAD_DIM)
    scaling = HEAD_DIM ** (-0.5)
    wide_in = stream.astype(jnp.float32)
    normal_one, inv_one = norm_parts(wide_in)
    normed1 = (normal_one * norm1_gain + norm1_bias).astype(jnp.bfloat16)
    projected = matmul(normed1, qkv_weight)
    query_rows = (projected[..., :model_width] + qv_bias[:model_width]).astype(jnp.bfloat16)
    key_rows = projected[..., model_width : 2 * model_width].astype(jnp.bfloat16)
    value_rows = (projected[..., 2 * model_width :] + qv_bias[model_width:]).astype(jnp.bfloat16)
    scores = (
        jnp.einsum(
            "bqhe,bkhe->bhqk",
            query_rows.reshape(heads_shape),
            key_rows.reshape(heads_shape),
            preferred_element_type=jnp.float32,
        )
        * scaling
    )
    top_score = jnp.max(scores, axis=-1, keepdims=True)
    exp_scores = jnp.exp(scores - top_score)
    totals = jnp.sum(exp_scores, axis=-1, keepdims=True)
    log_total = top_score + jnp.log(totals)
    attn_probs = (exp_scores / totals).astype(jnp.bfloat16)
    context = jnp.einsum(
        "bhqk,bkhe->bqhe",
        attn_probs,
        value_rows.reshape(heads_shape),
        preferred_element_type=jnp.float32,
    )
    context = context.reshape(images, length, model_width).astype(jnp.bfloat16)
    middle = wide_in + matmul(context, out_weight) + out_bias
    normal_two, inv_two = norm_parts(middle)
    normed2 = (normal_two * norm2_gain + norm2_bias).astype(jnp.bfloat16)
    pre_act = matmul(normed2, fc1_weight) + fc1_bias
    activated = gelu_value(pre_act).astype(jnp.bfloat16)
    result = live_scale * (middle + matmul(activated, fc2_weight) + fc2_bias)
    saved_inputs = (
        stream,
        query_rows,
        key_rows,
        value_rows,
        log_total,
        context,
        middle,
        pre_act,
        activated,
    )
    return (result.astype(jnp.bfloat16), saved_inputs)


def layer_backward(grad_out, live_scale, saved_inputs, params):
    (
        norm1_gain,
        norm1_bias,
        qkv_weight,
        qv_bias,
        out_weight,
        out_bias,
        norm2_gain,
        norm2_bias,
        fc1_weight,
        fc1_bias,
        fc2_weight,
        fc2_bias,
    ) = params
    stream, query_rows, key_rows, value_rows, log_total, context, middle, pre_act, activated = (
        saved_inputs
    )
    images, length, model_width = stream.shape
    heads_shape = (images, length, model_width // HEAD_DIM, HEAD_DIM)
    scaling = HEAD_DIM ** (-0.5)
    masked = live_scale * grad_out
    masked_half = masked.astype(jnp.bfloat16)
    grad_pre = transposed_product(masked_half, fc2_weight) * gelu_slope(pre_act)
    grad_pre_half = grad_pre.astype(jnp.bfloat16)
    grad_normed2 = transposed_product(grad_pre_half, fc1_weight)
    normal_two, inv_two = norm_parts(middle)
    grad_middle = masked + norm_back(grad_normed2 * norm2_gain, normal_two, inv_two)
    grad_middle_half = grad_middle.astype(jnp.bfloat16)
    grad_context = (
        transposed_product(grad_middle_half, out_weight).astype(jnp.bfloat16).reshape(heads_shape)
    )
    query_heads = query_rows.reshape(heads_shape)
    key_heads = key_rows.reshape(heads_shape)
    value_heads = value_rows.reshape(heads_shape)
    scores = (
        jnp.einsum("bqhe,bkhe->bhqk", query_heads, key_heads, preferred_element_type=jnp.float32)
        * scaling
    )
    probs_wide = jnp.exp(scores - log_total)
    probs_half = probs_wide.astype(jnp.bfloat16)
    grad_probs = jnp.einsum(
        "bqhe,bkhe->bhqk", grad_context, value_heads, preferred_element_type=jnp.float32
    )
    row_delta = jnp.sum(probs_wide * grad_probs, axis=-1, keepdims=True)
    grad_scores = (probs_wide * (grad_probs - row_delta) * scaling).astype(jnp.bfloat16)
    grad_query = jnp.einsum(
        "bhqk,bkhe->bqhe", grad_scores, key_heads, preferred_element_type=jnp.float32
    ).reshape(images, length, model_width)
    grad_keys = jnp.einsum(
        "bhqk,bqhe->bkhe", grad_scores, query_heads, preferred_element_type=jnp.float32
    ).reshape(images, length, model_width)
    grad_values = jnp.einsum(
        "bhqk,bqhe->bkhe", probs_half, grad_context, preferred_element_type=jnp.float32
    ).reshape(images, length, model_width)
    grad_proj = jnp.concatenate([grad_query, grad_keys, grad_values], axis=-1).astype(jnp.bfloat16)
    grad_normed1 = transposed_product(grad_proj, qkv_weight)
    wide_in = stream.astype(jnp.float32)
    normal_one, inv_one = norm_parts(wide_in)
    normed1 = (normal_one * norm1_gain + norm1_bias).astype(jnp.bfloat16)
    normed2 = (normal_two * norm2_gain + norm2_bias).astype(jnp.bfloat16)
    grad_stream = grad_middle + norm_back(grad_normed1 * norm1_gain, normal_one, inv_one)
    both_axes = (0, 1)
    scale_factors = (
        (normed1, grad_proj),
        (context, grad_middle_half),
        (normed2, grad_pre_half),
        (activated, masked_half),
    )
    vector_sums = (
        jnp.sum(grad_normed1 * normal_one, axis=both_axes),
        jnp.sum(grad_normed1, axis=both_axes),
        jnp.concatenate(
            [jnp.sum(grad_query, axis=both_axes), jnp.sum(grad_values, axis=both_axes)]
        ),
        jnp.sum(grad_middle, axis=both_axes),
        jnp.sum(grad_normed2 * normal_two, axis=both_axes),
        jnp.sum(grad_normed2, axis=both_axes),
        jnp.sum(grad_pre, axis=both_axes),
        jnp.sum(masked, axis=both_axes),
    )
    return (grad_stream, scale_factors, vector_sums)


def on_device(
    inputs,
    cotangent,
    live_slots,
    norm1_gain,
    norm1_bias,
    qkv_weight,
    qv_bias,
    out_weight,
    out_bias,
    norm2_gain,
    norm2_bias,
    fc1_weight,
    fc1_bias,
    fc2_weight,
    fc2_bias,
):
    is_first = lax.axis_index("section") == 0

    def per_section_values(toward_first_section, for_second):
        return jax.tree.map(
            lambda first_leaf, second_leaf: jnp.where(is_first, first_leaf, second_leaf),
            toward_first_section,
            for_second,
        )

    gathered = (
        lax.all_gather(norm1_gain, "dp", axis=1, tiled=True),
        lax.all_gather(norm1_bias, "dp", axis=1, tiled=True),
        lax.all_gather(qkv_weight, "dp", axis=1, tiled=True),
        lax.all_gather(qv_bias, "dp", axis=1, tiled=True),
        lax.all_gather(out_weight, "dp", axis=1, tiled=True),
        lax.all_gather(out_bias, "dp", axis=1, tiled=True),
        lax.all_gather(norm2_gain, "dp", axis=1, tiled=True),
        lax.all_gather(norm2_bias, "dp", axis=1, tiled=True),
        lax.all_gather(fc1_weight, "dp", axis=1, tiled=True),
        lax.all_gather(fc1_bias, "dp", axis=1, tiled=True),
        lax.all_gather(fc2_weight, "dp", axis=1, tiled=True),
        lax.all_gather(fc2_bias, "dp", axis=1, tiled=True),
    )
    params = tuple((member[0] for member in gathered))
    micro_count, slot_count, length, model_width = inputs.shape
    flat_shape = (micro_count * slot_count, length, model_width)
    live_scale = live_slots.reshape(-1).astype(jnp.float32)[:, None, None]
    early_result, early_saved = layer_forward(inputs.reshape(flat_shape), live_scale, params)
    received = passed_along(early_result, "section", 1)
    late_result, late_saved = layer_forward(received, live_scale, params)
    block_outs = per_section_values(early_result, late_result)
    saved_inputs = per_section_values(early_saved, late_saved)
    top_grad = cotangent.reshape(flat_shape).astype(jnp.float32)
    early_back, early_factors, early_sums = layer_backward(
        top_grad, live_scale, saved_inputs, params
    )
    received_grad = passed_along(early_back.astype(jnp.bfloat16), "section", -1).astype(
        early_back.dtype
    )
    late_back, late_factors, late_sums = layer_backward(
        received_grad, live_scale, saved_inputs, params
    )
    grad_stream = per_section_values(late_back, early_back)
    valid_factors = per_section_values(late_factors, early_factors)
    valid_sums = per_section_values(late_sums, early_sums)

    def outer_sum(position):
        left_rows, right_rows = valid_factors[position]
        return jnp.einsum("bsd,bse->de", left_rows, right_rows, preferred_element_type=jnp.float32)[
            None
        ]

    def vector_total(position):
        return valid_sums[position][None]

    mlp_parts = (
        lax.psum_scatter(vector_total(4), "dp", scatter_dimension=1, tiled=True),
        lax.psum_scatter(vector_total(5), "dp", scatter_dimension=1, tiled=True),
        lax.psum_scatter(outer_sum(2), "dp", scatter_dimension=1, tiled=True),
        lax.psum_scatter(vector_total(6), "dp", scatter_dimension=1, tiled=True),
        lax.psum_scatter(outer_sum(3), "dp", scatter_dimension=1, tiled=True),
        lax.psum_scatter(vector_total(7), "dp", scatter_dimension=1, tiled=True),
    )
    attn_parts = (
        lax.psum_scatter(vector_total(0), "dp", scatter_dimension=1, tiled=True),
        lax.psum_scatter(vector_total(1), "dp", scatter_dimension=1, tiled=True),
        lax.psum_scatter(outer_sum(0), "dp", scatter_dimension=1, tiled=True),
        lax.psum_scatter(vector_total(2), "dp", scatter_dimension=1, tiled=True),
        lax.psum_scatter(outer_sum(1), "dp", scatter_dimension=1, tiled=True),
        lax.psum_scatter(vector_total(3), "dp", scatter_dimension=1, tiled=True),
    )
    outputs = block_outs.reshape(inputs.shape)[None]
    in_grads = grad_stream.reshape(inputs.shape)[None]
    return (
        outputs,
        in_grads,
        attn_parts[0],
        attn_parts[1],
        attn_parts[2],
        attn_parts[3],
        attn_parts[4],
        attn_parts[5],
        mlp_parts[0],
        mlp_parts[1],
        mlp_parts[2],
        mlp_parts[3],
        mlp_parts[4],
        mlp_parts[5],
    )


def solution(mesh):
    in_specs = (
        P(None, "dp", None, None),
        P(None, "dp", None, None),
        P(None, "dp"),
        P("section", "dp"),
        P("section", "dp"),
        P("section", "dp", None),
        P("section", "dp"),
        P("section", "dp", None),
        P("section", "dp"),
        P("section", "dp"),
        P("section", "dp"),
        P("section", "dp", None),
        P("section", "dp"),
        P("section", "dp", None),
        P("section", "dp"),
    )
    out_specs = (
        P("section", None, "dp", None, None),
        P("section", None, "dp", None, None),
        P("section", "dp"),
        P("section", "dp"),
        P("section", "dp", None),
        P("section", "dp"),
        P("section", "dp", None),
        P("section", "dp"),
        P("section", "dp"),
        P("section", "dp"),
        P("section", "dp", None),
        P("section", "dp"),
        P("section", "dp", None),
        P("section", "dp"),
    )
    return jax.shard_map(
        on_device, mesh=mesh, in_specs=in_specs, out_specs=out_specs, check_vma=False
    )
```

profile of v0, /device:TPU:0, one launch (start us, length us, event | category | flops | bytes accessed | tf_op | source)
XLA Modules:
  0.0 1431.4 jit_solution(4565727010739830815)
XLA Ops:
  17.0 65.1 %all-reduce.6 = (bf16[1024]{0:T(1024)(128)(2,1)S(1)}, bf16[1024]{0:T(1024)(128)(2,1)S(1)}, bf16[1024]{0:T(1024)(128)(2,1)S(1)}, bf16[1024]{0:T(1024)(128)(2,1)S(...) all-reduce(bf16[1024]{0:T(1024)(128)(2,1)S(1)} %dynamic-update-slic, ...), channel_id=1, replica_groups=mesh['section'=2,'dp'=16] {'dp'}, use_global_device_ids=true, to_apply=%add.1 | all-reduce | flops 6144 | bytes 24576
  82.1 17.5 %all_gather.45 = bf16[1,4096]{1,0:T(2,128)(2,1)S(1)} all-gather(bf16[1,256]{1,0:T(2,128)(2,1)} %param.27), channel_id=1, replica_groups=mesh['section'=2,'dp'=16] {'dp'}, dimensions={1}, use_global_device_ids=true | all-gather | bytes 8704 | tf_op jit(solution)/shard_map/all_gather | solution.py:238
  99.6 19.3 %all_gather.39 = bf16[1,2048]{1,0:T(2,128)(2,1)S(1)} all-gather(bf16[1,128]{1,0:T(2,128)(2,1)} %param.21), channel_id=1, replica_groups=mesh['section'=2,'dp'=16] {'dp'}, dimensions={1}, use_global_device_ids=true | all-gather | bytes 4352 | tf_op jit(solution)/shard_map/all_gather | solution.py:232
  130.0 62.7 %all-gather.9.cloned.1.call-done = bf16[1,1024,4096]{2,1,0:T(8,128)(2,1)} async-done(((bf16[1,64,4096]{2,1,0:T(8,128)(2,1)}), bf16[1,1024,4096]{2,1,0:T(8,128)(2,1)}) %all-gather.9.cloned.1.call-update) | async-done | bytes 8388624 | tf_op jit(solution)/shard_map/all_gather | solution.py:237
  197.4 70.2 %all-gather.11.cloned.1.call-done = bf16[1,4096,1024]{2,1,0:T(8,128)(2,1)} async-done(((bf16[1,256,1024]{2,1,0:T(8,128)(2,1)}), bf16[1,4096,1024]{2,1,0:T(8,128)(2,1)}) %all-gather.11.cloned.1.call-update) | async-done | bytes 8388624 | tf_op jit(solution)/shard_map/all_gather | solution.py:239
  297.8 6.2 fusion.29
  338.2 6.1 fusion.150
  347.2 9.4 collective-permute-done.1
  356.6 6.7 fusion.269
  385.8 6.5 fusion.149
  403.5 6.4 convolution_bitcast_fusion.2
  411.6 9.9 convolution_bitcast_fusion
  423.0 8.2 convolution_bitcast_fusion.1
  441.1 46.9 %reduce-scatter.45.cloned.1.call-done = f32[64,1]{1,0:T(8,128)} async-done(((f32[1024,1]{1,0:T(8,128)}), f32[64,1]{1,0:T(8,128)}) %reduce-scatter.45.cloned.1.call-update) | async-done | bytes 272
  489.3 57.5 %reduce-scatter.47.cloned.1.call-done = f32[64,1]{1,0:T(8,128)} async-done(((f32[1024,1]{1,0:T(8,128)}), f32[64,1]{1,0:T(8,128)}) %reduce-scatter.47.cloned.1.call-update) | async-done | bytes 272
  548.1 57.4 %reduce-scatter.37.cloned.1.call-done = f32[64,1]{1,0:T(8,128)} async-done(((f32[1024,1]{1,0:T(8,128)}), f32[64,1]{1,0:T(8,128)}) %reduce-scatter.37.cloned.1.call-update) | async-done | bytes 272
  606.9 57.5 %reduce-scatter.39.cloned.1.call-done = f32[64,1]{1,0:T(8,128)} async-done(((f32[1024,1]{1,0:T(8,128)}), f32[64,1]{1,0:T(8,128)}) %reduce-scatter.39.cloned.1.call-update) | async-done | bytes 272
  665.7 57.3 %reduce-scatter.43.cloned.1.call-done = f32[64,1]{1,0:T(8,128)} async-done(((f32[1024,1]{1,0:T(8,128)}), f32[64,1]{1,0:T(8,128)}) %reduce-scatter.43.cloned.1.call-update) | async-done | bytes 272
  724.4 58.9 %reduce-scatter.41.cloned.1.call-done = f32[128,1]{1,0:T(8,128)} async-done(((f32[2048,1]{1,0:T(8,128)}), f32[128,1]{1,0:T(8,128)}) %reduce-scatter.41.cloned.1.call-update) | async-done | bytes 528
  784.7 63.1 %reduce-scatter.49.cloned.1.call-done = f32[256,1]{1,0:T(8,128)} async-done(((f32[4096,1]{1,0:T(8,128)}), f32[256,1]{1,0:T(8,128)}) %reduce-scatter.49.cloned.1.call-update) | async-done | bytes 1040
  849.3 74.7 %reduce-scatter.31.cloned.1.call-done = f32[1,64,1024]{2,1,0:T(8,128)} async-done(((f32[1,1024,1024]{2,1,0:T(8,128)}), f32[1,64,1024]{2,1,0:T(8,128)}) %reduce-scatter.31.cloned.1.call-update) | async-done | bytes 262160 | tf_op jit(solution)/shard_map/reduce_scatter | solution.py:287
  924.0 138.5 %reduce-scatter.29.cloned.1.call-done = f32[1,64,3072]{2,1,0:T(8,128)} async-done(((f32[1,1024,3072]{2,1,0:T(8,128)}), f32[1,64,3072]{2,1,0:T(8,128)}) %reduce-scatter.29.cloned.1.call-update) | async-done | bytes 786448 | tf_op jit(solution)/shard_map/reduce_scatter | solution.py:285
  1062.5 181.2 %reduce-scatter.35.cloned.1.call-done = f32[1,256,1024]{2,1,0:T(8,128)} async-done(((f32[1,4096,1024]{2,1,0:T(8,128)}), f32[1,256,1024]{2,1,0:T(8,128)}) %reduce-scatter.35.cloned.1.call-update) | async-done | bytes 1048592 | tf_op jit(solution)/shard_map/reduce_scatter | solution.py:279
  1243.7 181.0 %reduce-scatter.33.cloned.1.call-done = f32[1,64,4096]{2,1,0:T(8,128)} async-done(((f32[1,1024,4096]{2,1,0:T(8,128)}), f32[1,64,4096]{2,1,0:T(8,128)}) %reduce-scatter.33.cloned.1.call-update) | async-done | bytes 1048592 | tf_op jit(solution)/shard_map/reduce_scatter | solution.py:277
  (283 shorter events, 147.5 us)
Async XLA Ops:
  7.2 112.8 %copy-start.14 = (bf16[2,1,64,1024]{3,2,1,0:T(8,128)(2,1)S(1)}, bf16[2,1,64,1024]{3,2,1,0:T(8,128)(2,1)}, u32[]{:S(2)}) copy-start(bf16[2,1,64,1024]{3,2,1,0:T(8,128)(2,1)} %param.15) | copy-start | bytes 786436
  7.2 113.0 %copy-start.48 = (s32[2,1]{0,1:T(1,128)S(1)}, s32[2,1]{0,1:T(1,128)}, u32[]{:S(2)}) copy-start(s32[2,1]{0,1:T(1,128)} %param.17) | copy-start | bytes 28
  7.2 113.0 %all-gather.5.cloned.1.call-start = ((), (), s32[]{:S(2)}) async-start(), calls=%async_computation.12 | async-start | bytes 6684672 | tf_op jit(solution)/shard_map/all_gather | solution.py:231
  7.9 119.5 %all-gather.7.cloned.1.call-start = ((), (), s32[]{:S(2)}) async-start(), calls=%async_computation.13 | async-start | bytes 2228224 | tf_op jit(solution)/shard_map/all_gather | solution.py:233
  8.7 184.0 %all-gather.9.cloned.1.call-start = ((), (), s32[]{:S(2)}) async-start(), calls=%async_computation.14 | async-start | bytes 8912896 | tf_op jit(solution)/shard_map/all_gather | solution.py:237
  9.4 258.2 %all-gather.11.cloned.1.call-start = ((), (), s32[]{:S(2)}) async-start(), calls=%async_computation.15 | async-start | bytes 8912896 | tf_op jit(solution)/shard_map/all_gather | solution.py:239
  10.0 429.7 %reduce-scatter.51.cloned.1.call-start = ((), (), s32[]{:S(2)}) async-start(), calls=%async_computation.27 | async-start | bytes 557056
  127.4 65.3 %copy-start.41 = (bf16[2,16,64,64]{3,2,1,0:T(8,128)(2,1)}, bf16[2,16,64,64]{3,2,1,0:T(8,128)(2,1)S(1)}, u32[]{:S(2)}) copy-start(bf16[2,16,64,64]{3,2,1,0:T(8,128)(2,1)S(1)} %convolution_convert_fusion.3) | copy-start | bytes 786436
  197.4 74.9 %copy-start.1 = (f32[2,64,4096]{2,1,0:T(8,128)}, f32[2,64,4096]{2,1,0:T(8,128)S(1)}, u32[]{:S(2)}) copy-start(f32[2,64,4096]{2,1,0:T(8,128)S(1)} %fusion.26) | copy-start | bytes 6291460
  272.4 9.3 collective-permute-start
  338.2 18.4 %copy-start.3 = (f32[2,64,4096]{2,1,0:T(8,128)S(1)}, f32[2,64,4096]{2,1,0:T(8,128)}, u32[]{:S(2)}) copy-start(f32[2,64,4096]{2,1,0:T(8,128)} %copy-done.1) | copy-start | bytes 6291460
  338.2 18.4 %copy-start.5 = (f32[2,64,4096]{2,1,0:T(8,128)S(1)}, f32[2,64,4096]{2,1,0:T(8,128)}, u32[]{:S(2)}) copy-start(f32[2,64,4096]{2,1,0:T(8,128)} %fusion.29) | copy-start | bytes 6291460
  345.4 11.2 collective-permute-start.1
  375.3 112.7 %reduce-scatter.45.cloned.1.call-start = ((), (), s32[]{:S(2)}) async-start(), calls=%async_computation.24 | async-start | bytes 557056
  379.2 167.6 %reduce-scatter.47.cloned.1.call-start = ((), (), s32[]{:S(2)}) async-start(), calls=%async_computation.25 | async-start | bytes 557056
  385.8 219.8 %reduce-scatter.37.cloned.1.call-start = ((), (), s32[]{:S(2)}) async-start(), calls=%async_computation.20 | async-start | bytes 557056
  393.4 271.0 %reduce-scatter.39.cloned.1.call-start = ((), (), s32[]{:S(2)}) async-start(), calls=%async_computation.21 | async-start | bytes 557056
  394.5 328.5 %reduce-scatter.43.cloned.1.call-start = ((), (), s32[]{:S(2)}) async-start(), calls=%async_computation.23 | async-start | bytes 557056
  395.9 387.3 %reduce-scatter.41.cloned.1.call-start = ((), (), s32[]{:S(2)}) async-start(), calls=%async_computation.22 | async-start | bytes 1114112
  397.4 450.4 %reduce-scatter.49.cloned.1.call-start = ((), (), s32[]{:S(2)}) async-start(), calls=%async_computation.26 | async-start | bytes 2228224
  399.7 524.4 %reduce-scatter.31.cloned.1.call-start = ((), (), s32[]{:S(2)}) async-start(), calls=%async_computation.17 | async-start | bytes 4456448 | tf_op jit(solution)/shard_map/reduce_scatter | solution.py:287
  402.5 660.0 %reduce-scatter.29.cloned.1.call-start = ((), (), s32[]{:S(2)}) async-start(), calls=%async_computation.16 | async-start | bytes 13369344 | tf_op jit(solution)/shard_map/reduce_scatter | solution.py:285
  410.0 833.7 %reduce-scatter.35.cloned.1.call-start = ((), (), s32[]{:S(2)}) async-start(), calls=%async_computation.19 | async-start | bytes 17825792 | tf_op jit(solution)/shard_map/reduce_scatter | solution.py:279
  421.5 1003.2 %reduce-scatter.33.cloned.1.call-start = ((), (), s32[]{:S(2)}) async-start(), calls=%async_computation.18 | async-start | bytes 17825792 | tf_op jit(solution)/shard_map/reduce_scatter | solution.py:277
  (49 other events, 215.2 us)
Sparse Core Ops, SparseCore 0:
  10.3 64.6 all-gather.4
  77.1 40.2 all-gather.6
  119.6 72.9 all-gather.8
  194.7 72.8 all-gather.10
  375.4 53.9 reduce-scatter.50
  432.8 55.1 reduce-scatter.44
  491.5 55.2 reduce-scatter.46
  550.3 55.1 reduce-scatter.36
  609.1 55.1 reduce-scatter.38
  667.8 55.2 reduce-scatter.42
  726.7 56.5 reduce-scatter.40
  786.9 60.8 reduce-scatter.48
  852.2 71.8 reduce-scatter.30
  928.5 133.9 reduce-scatter.28
  1067.0 176.5 reduce-scatter.34
  1248.2 176.4 reduce-scatter.32
where the time goes:
time: 1440 us; the launch traced here: 1430 us
  waiting for transfers between devices  1120 us (78%)
  matrix products  116 us (8%)
  blocking collectives  102 us (7%)
  local copies, waits for them, and re-layouts  60.2 us (4%)
  between operations  15.8 us (1%)
    unnamed x24, waiting for transfers between devices  401 us
    reduce_scatter x1, waiting for transfers between devices, on_device(): lax.psum_scatter(outer_sum(3), 'dp', scatter_dimension=1, tiled=True)  181 us
    reduce_scatter x1, waiting for transfers between devices, on_device(): lax.psum_scatter(outer_sum(2), 'dp', scatter_dimension=1, tiled=True)  181 us
    reduce_scatter x1, waiting for transfers between devices, on_device(): lax.psum_scatter(outer_sum(0), 'dp', scatter_dimension=1, tiled=True)  138 us
    reduce_scatter x1, waiting for transfers between devices, on_device(): lax.psum_scatter(outer_sum(1), 'dp', scatter_dimension=1, tiled=True)  74.7 us
    all_gather x1, waiting for transfers between devices, on_device(): lax.all_gather(fc2_weight, 'dp', axis=1, tiled=True)  70.2 us
    unnamed x1, blocking collectives  65.1 us
    all_gather x1, waiting for transfers between devices, on_device(): lax.all_gather(fc1_weight, 'dp', axis=1, tiled=True)  62.7 us
  transfers between devices with their start and end apart: 18, of which 15 were waited for; matrix products, arithmetic and copies ran while one was open for 6% of the time, Pallas kernels for 0%

commit v1 on v0

--- a/solution.py
+++ b/solution.py
@@ -4,6 +4,7 @@
 from jax.sharding import PartitionSpec as P
 
 HEAD_DIM = 64
+LANES = 128
 
 
 EPSILON = 1e-06
@@ -217,93 +218,86 @@
     fc2_bias,
 ):
     is_first = lax.axis_index("section") == 0
-
-    def per_section_values(toward_first_section, for_second):
-        return jax.tree.map(
-            lambda first_leaf, second_leaf: jnp.where(is_first, first_leaf, second_leaf),
-            toward_first_section,
-            for_second,
-        )
-
-    gathered = (
-        lax.all_gather(norm1_gain, "dp", axis=1, tiled=True),
-        lax.all_gather(norm1_bias, "dp", axis=1, tiled=True),
-        lax.all_gather(qkv_weight, "dp", axis=1, tiled=True),
-        lax.all_gather(qv_bias, "dp", axis=1, tiled=True),
-        lax.all_gather(out_weight, "dp", axis=1, tiled=True),
-        lax.all_gather(out_bias, "dp", axis=1, tiled=True),
-        lax.all_gather(norm2_gain, "dp", axis=1, tiled=True),
-        lax.all_gather(norm2_bias, "dp", axis=1, tiled=True),
-        lax.all_gather(fc1_weight, "dp", axis=1, tiled=True),
-        lax.all_gather(fc1_bias, "dp", axis=1, tiled=True),
-        lax.all_gather(fc2_weight, "dp", axis=1, tiled=True),
-        lax.all_gather(fc2_bias, "dp", axis=1, tiled=True),
-    )
-    params = tuple((member[0] for member in gathered))
     micro_count, slot_count, length, model_width = inputs.shape
     flat_shape = (micro_count * slot_count, length, model_width)
+    small_shards = [
+        norm1_gain[0], norm1_bias[0], qv_bias[0], out_bias[0],
+        norm2_gain[0], norm2_bias[0], fc1_bias[0], fc2_bias[0],
+    ]
+    rows = qkv_weight.shape[1]
+    small_sizes = [shard.shape[0] for shard in small_shards]
+    per_row = sum(small_sizes) // rows
+    small_pad = -per_row % LANES
+    packed_small = jnp.pad(
+        jnp.concatenate(small_shards).reshape(rows, per_row), ((0, 0), (0, small_pad))
+    )
+    qkv_width = qkv_weight.shape[2]
+    head_width = qkv_width + out_weight.shape[2]
+    attn_shard = jnp.concatenate([qkv_weight[0], out_weight[0], packed_small], axis=1)
+    attn_all = lax.all_gather(attn_shard, "dp", axis=0, tiled=True)
+    full_fc1 = lax.all_gather(fc1_weight[0], "dp", axis=0, tiled=True)
+    full_fc2 = lax.all_gather(fc2_weight[0], "dp", axis=0, tiled=True)
+    small_all = attn_all[:, head_width : head_width + per_row].reshape(-1, sum(small_sizes))
+    small_full, begin = [], 0
+    for size in small_sizes:
+        small_full.append(small_all[:, begin : begin + size].reshape(-1))
+        begin += size
+    params = (
+        small_full[0], small_full[1], attn_all[:, :qkv_width], small_full[2],
+        attn_all[:, qkv_width:head_width], small_full[3], small_full[4], small_full[5],
+        full_fc1, small_full[6], full_fc2, small_full[7],
+    )
     live_scale = live_slots.reshape(-1).astype(jnp.float32)[:, None, None]
-    early_result, early_saved = layer_forward(inputs.reshape(flat_shape), live_scale, params)
+    flat_inputs = inputs.reshape(flat_shape)
+    early_result, _ = layer_forward(flat_inputs, live_scale, params)
     received = passed_along(early_result, "section", 1)
-    late_result, late_saved = layer_forward(received, live_scale, params)
-    block_outs = per_section_values(early_result, late_result)
-    saved_inputs = per_section_values(early_saved, late_saved)
-    top_grad = cotangent.reshape(flat_shape).astype(jnp.float32)
-    early_back, early_factors, early_sums = layer_backward(
-        top_grad, live_scale, saved_inputs, params
-    )
-    received_grad = passed_along(early_back.astype(jnp.bfloat16), "section", -1).astype(
-        early_back.dtype
-    )
-    late_back, late_factors, late_sums = layer_backward(
-        received_grad, live_scale, saved_inputs, params
-    )
-    grad_stream = per_section_values(late_back, early_back)
-    valid_factors = per_section_values(late_factors, early_factors)
-    valid_sums = per_section_values(late_sums, early_sums)
+    stream = jnp.where(is_first, flat_inputs, received)
+    result, saved_inputs = layer_forward(stream, live_scale, params)
+    top_grad = cotangent.reshape(flat_shape)
+    early_back, _, _ = layer_backward(
+        top_grad.astype(jnp.float32), live_scale, saved_inputs, params
+    )
+    received_grad = passed_along(early_back.astype(jnp.bfloat16), "section", -1)
+    own_grad = jnp.where(is_first, received_grad, top_grad).astype(jnp.float32)
+    grad_stream, factors, sums = layer_backward(own_grad, live_scale, saved_inputs, params)
 
     def outer_sum(position):
-        left_rows, right_rows = valid_factors[position]
-        return jnp.einsum("bsd,bse->de", left_rows, right_rows, preferred_element_type=jnp.float32)[
-            None
-        ]
-
-    def vector_total(position):
-        return valid_sums[position][None]
-
-    mlp_parts = (
-        lax.psum_scatter(vector_total(4), "dp", scatter_dimension=1, tiled=True),
-        lax.psum_scatter(vector_total(5), "dp", scatter_dimension=1, tiled=True),
-        lax.psum_scatter(outer_sum(2), "dp", scatter_dimension=1, tiled=True),
-        lax.psum_scatter(vector_total(6), "dp", scatter_dimension=1, tiled=True),
-        lax.psum_scatter(outer_sum(3), "dp", scatter_dimension=1, tiled=True),
-        lax.psum_scatter(vector_total(7), "dp", scatter_dimension=1, tiled=True),
-    )
-    attn_parts = (
-        lax.psum_scatter(vector_total(0), "dp", scatter_dimension=1, tiled=True),
-        lax.psum_scatter(vector_total(1), "dp", scatter_dimension=1, tiled=True),
-        lax.psum_scatter(outer_sum(0), "dp", scatter_dimension=1, tiled=True),
-        lax.psum_scatter(vector_total(2), "dp", scatter_dimension=1, tiled=True),
-        lax.psum_scatter(outer_sum(1), "dp", scatter_dimension=1, tiled=True),
-        lax.psum_scatter(vector_total(3), "dp", scatter_dimension=1, tiled=True),
-    )
-    outputs = block_outs.reshape(inputs.shape)[None]
-    in_grads = grad_stream.reshape(inputs.shape)[None]
+        left_rows, right_rows = factors[position]
+        return jnp.einsum(
+            "bsd,bse->de", left_rows, right_rows, preferred_element_type=jnp.float32
+        ).astype(jnp.bfloat16)
+
+    def scattered(partial):
+        return lax.psum_scatter(partial, "dp", scatter_dimension=0, tiled=True).astype(jnp.float32)
+
+    fc2_grad = scattered(outer_sum(3))
+    fc1_grad = scattered(outer_sum(2))
+    shares = model_width // rows
+    small_sums = jnp.concatenate(
+        [total.reshape(shares, size) for total, size in zip(sums, small_sizes)], axis=1
+    ).reshape(model_width, per_row)
+    small_sums = jnp.pad(small_sums, ((0, 0), (0, small_pad))).astype(jnp.bfloat16)
+    attn_grad = scattered(jnp.concatenate([outer_sum(0), outer_sum(1), small_sums], axis=1))
+    small_flat = attn_grad[:, head_width : head_width + per_row].reshape(-1)
+    small_grads, begin = [], 0
+    for size in small_sizes:
+        small_grads.append(small_flat[begin : begin + size][None])
+        begin += size
     return (
-        outputs,
-        in_grads,
-        attn_parts[0],
-        attn_parts[1],
-        attn_parts[2],
-        attn_parts[3],
-        attn_parts[4],
-        attn_parts[5],
-        mlp_parts[0],
-        mlp_parts[1],
-        mlp_parts[2],
-        mlp_parts[3],
-        mlp_parts[4],
-        mlp_parts[5],
+        result.reshape(inputs.shape)[None],
+        grad_stream.reshape(inputs.shape)[None],
+        small_grads[0],
+        small_grads[1],
+        attn_grad[None, :, :qkv_width],
+        small_grads[2],
+        attn_grad[None, :, qkv_width:head_width],
+        small_grads[3],
+        small_grads[4],
+        small_grads[5],
+        fc1_grad[None],
+        small_grads[6],
+        fc2_grad[None],
+        small_grads[7],
     )
 
 

time: 1440 us -> 669 us (0.46)
  waiting for transfers between devices: 1120 us -> 474 us
  blocking collectives: 102 us -> 0 us
  local copies, waits for them, and re-layouts: 60.2 us -> 35.8 us
    unnamed x24 -> x6, waiting for transfers between devices: 401 us -> 1.44 us
    reduce_scatter x4 -> x3, waiting for transfers between devices: 575 us -> 242 us  [scattered(): lax.psum_scatter(partial, 'dp', scatter_dimension=0, tiled=True)]
    all_gather x4 -> x3, waiting for transfers between devices: 133 us -> 216 us  [the longest x1 76.9 us: on_device(): attn_all = lax.all_gather(attn_shard, 'dp', axis=0, tiled=True)]
    unnamed x1 -> x0, blocking collectives: 65.1 us -> none
    all_gather x2 -> x0, blocking collectives: 36.7 us -> none  [the longest x1 19.3 us: on_device(): lax.all_gather(qv_bias, 'dp', axis=1, tiled=True)]
    unnamed x139 -> x41, local copies, waits for them, and re-layouts: 36.4 us -> 1.33 us
    dot_general x8 -> x7, matrix products: 32.5 us -> 44.9 us  [transposed_product(): jnp.einsum('bse,de->bsd', left_rows, weight, preferred_element_type=jnp.f...]
    dot_general x8 -> x7, matrix products: 32 us -> 31.3 us  [matmul(): jnp.einsum('bsd,de->bse', left_rows, weight, preferred_element_type=jnp.f...]
  transfers between devices with their start and end apart: 18 -> 8, of which waited for: 15 -> 8; matrix products, arithmetic and copies ran while one was open for 6% -> 13% of each run, Pallas kernels for 0% -> 0%
where the time goes in v1:
time: 669 us; the launch traced here: 662 us
  waiting for transfers between devices  474 us (71%)
  matrix products  116 us (17%)
  local copies, waits for them, and re-layouts  35.8 us (5%)
  other arithmetic  15.3 us (2%)
  between operations  15.1 us (2%)
    reduce_scatter x3, waiting for transfers between devices, scattered(): lax.psum_scatter(partial, 'dp', scatter_dimension=0, tiled=True)  242 us
    all_gather x1, waiting for transfers between devices, on_device(): attn_all = lax.all_gather(attn_shard, 'dp', axis=0, tiled=True)  76.9 us
    all_gather x1, waiting for transfers between devices, on_device(): full_fc1 = lax.all_gather(fc1_weight[0], 'dp', axis=0, tiled=True)  75.1 us
    all_gather x1, waiting for transfers between devices, on_device(): full_fc2 = lax.all_gather(fc2_weight[0], 'dp', axis=0, tiled=True)  64.4 us
    dot_general x7, matrix products, transposed_product(): jnp.einsum('bse,de->bsd', left_rows, weight, preferred_element_type=jnp.f...  44.9 us
    dot_general x7, matrix products, matmul(): jnp.einsum('bsd,de->bse', left_rows, weight, preferred_element_type=jnp.f...  31.3 us
    dot_general x4, matrix products, outer_sum(): jnp.einsum('bsd,bse->de', left_rows, right_rows, preferred_element_type=j...  14.6 us
    ppermute x2, waiting for transfers between devices, passed_along(): lax.ppermute(value, axis, [(source, source + steps) for source in range(l...  14.1 us
  transfers between devices with their start and end apart: 8, of which 8 were waited for; matrix products, arithmetic and copies ran while one was open for 13% of the time, Pallas kernels for 0%

profile of v1, /device:TPU:0, one launch (start us, length us, event | category | flops | bytes accessed | tf_op | source)
XLA Modules:
  0.0 661.6 jit_solution(4163150427755503981)
XLA Ops:
  8.0 4.8 concatenate.30
  16.7 76.9 %all-gather.6.cloned.1.call-done = bf16[1024,4224]{1,0:T(8,128)(2,1)} async-done(((bf16[64,4224]{1,0:T(8,128)(2,1)}), bf16[1024,4224]{1,0:T(8,128)(2,1)}) %all-gather.6.cloned.1.call-update) | async-done | bytes 8650768 | tf_op jit(solution)/shard_map/all_gather | solution.py:237
  95.2 3.9 fusion.45
  104.3 64.4 %all-gather.10.cloned.1.call-done = bf16[1,4096,1024]{2,1,0:T(8,128)(2,1)} async-done(((bf16[1,256,1024]{2,1,0:T(8,128)(2,1)}), bf16[1,4096,1024]{2,1,0:T(8,128)(2,1)}) %all-gather.10.cloned.1.call-update) | async-done | bytes 8388624 | tf_op jit(solution)/shard_map/all_gather | solution.py:239
  168.7 75.1 %all-gather.8.cloned.1.call-done = bf16[1,1024,4096]{2,1,0:T(8,128)(2,1)} async-done(((bf16[1,64,4096]{2,1,0:T(8,128)(2,1)}), bf16[1,1024,4096]{2,1,0:T(8,128)(2,1)}) %all-gather.8.cloned.1.call-update) | async-done | bytes 8388624 | tf_op jit(solution)/shard_map/all_gather | solution.py:238
  243.8 8.6 %fusion.80 = bf16[2,64,1024]{2,1,0:T(8,128)(2,1)S(1)} fusion(f32[2,64,1024]{2,1,0:T(8,128)S(1)} %get-tuple-element.83, bf16[1,4096,1024]{2,1,0:T(8,128)(2,1)} %all-gather.10.cloned.1.call-done, bf16[1,1024,4096]{2,1,0:T(8,128)(2,1)} %all-gather.8.cloned.1.call-done, f32[4096]{0:T(1024)S(1)} %bitcast.233, f32[1024]{0:T(1024)S(1)} %reshape.351, ...), kind=kOutput, calls=%fused_computation.77 | convolution fusion | flops 2151809024 | bytes 17593352 | tf_op jit(solution)/shard_map/bsd,de->bse/dot_general | solution.py:46
  255.9 5.8 collective-permute-done
  262.1 3.9 fusion.44
  271.0 4.7 fusion.24
  275.7 12.4 %fusion.221 = (f32[2,64]{1,0:T(2,128)S(1)}, f32[2,64]{1,0:T(2,128)S(1)}, f32[2,64,1024]{2,1,0:T(8,128)}) fusion(f32[2,64]{1,0:T(2,128)S(1)} %add_rsqrt_fusion, f32[2,64,1024]{2,1,0:T(8,128)S(1)} %get-tuple-element.87, f32[2,64]{1,0:T(2,128)S(1)} %broadcast_multiply_fusion.8, f32[1024]{0:T(1024)S(1)} %reshape.348, ...), kind=kOutput, calls=%fused_computation.261 | convolution fusion | flops 2153906176 | bytes 20191240 | tf_op jit(solution)/shard_map/bse,de->bsd/dot_general | solution.py:50
  297.2 4.0 convolution_convert_fusion.2
  310.9 5.4 fusion.220
  318.1 8.3 %collective-permute-done.1 = bf16[2,64,1024]{2,1,0:T(8,128)(2,1)S(1)} collective-permute-done((bf16[2,64,1024]{2,1,0:T(8,128)(2,1)S(1)}, bf16[2,64,1024]{2,1,0:T(8,128)(2,1)S(1)}, u32[]{:S(2)}, u32[]{:S(2)}) %collective-permute-start.1) | collective-permute-done | bytes 262176 | tf_op jit(solution)/shard_map/ppermute | solution.py:18
  326.6 4.7 bitcast_convert_fusion
  331.3 6.7 %fusion.239 = (bf16[4096]{0:T(1024)(128)(2,1)S(1)}, bf16[2,64,4096]{2,1,0:T(8,128)(2,1)S(1)}) fusion(f32[2,64,4096]{2,1,0:T(8,128)S(1)} %fusion.24, bf16[1,4096,1024]{2,1,0:T(8,128)(2,1)} %all-gather.10.cloned.1.call-done, bf16[2,64,1024]{2,1,0:T(8,128)(2,1)S(1)} %get-tuple-element.55, f32[2]{0:T(128)S(1)} %convert_bitcast_fusion.1), kind=kOutput, calls=%fused_computation.269 | convolution fusion | flops 1079898112 | bytes 11804680 | tf_op jit(solution)/shard_map/bse,de->bsd/dot_general | solution.py:50
  338.9 6.2 bitcast_convert_fusion.1
  345.5 7.7 %multiply_reduce_fusion.2 = (bf16[1024]{0:T(1024)(128)(2,1)S(1)}, f32[2,64]{1,0:T(2,128)S(1)}, f32[2,64]{1,0:T(2,128)S(1)}, bf16[1024]{0:T(1024)(128)(2,1)S(1)}, f32[2,64,1024]{2,1,0:T(8,128)S(1)}) fusion(f32[2,64]{1,0:T(2,128)S(1)} %add_rsqrt_fusion, f32[2,64,1024]{2,1,0:T(8,128)S(1)} %get-tuple-element.87, f32[2,64]{1,0:T(2,128)S(1)} %broadcast_multiply_fusion.8, ...), kind=kOutput, calls=%fused_computation.149 | convolution fusion | flops 1074919168 | bytes 10496000 | tf_op jit(solution)/shard_map/bse,de->bsd/dot_general | solution.py:50
  366.3 3.9 convolution_convert_fusion
  372.2 4.0 fusion.223
  380.5 6.2 fusion.131
  396.3 5.6 fusion.86
  403.0 29.5 %reduce-scatter.8.cloned.1.call-done = bf16[256,1024]{1,0:T(8,128)(2,1)} async-done(((bf16[4096,1024]{1,0:T(8,128)(2,1)}), bf16[256,1024]{1,0:T(8,128)(2,1)}) %reduce-scatter.8.cloned.1.call-update) | async-done | bytes 524304 | tf_op jit(solution)/shard_map/reduce_scatter | solution.py:271
  434.7 104.9 %reduce-scatter.6.cloned.1.call-done = bf16[64,4096]{1,0:T(8,128)(2,1)} async-done(((bf16[1024,4096]{1,0:T(8,128)(2,1)}), bf16[64,4096]{1,0:T(8,128)(2,1)}) %reduce-scatter.6.cloned.1.call-update) | async-done | bytes 524304 | tf_op jit(solution)/shard_map/reduce_scatter | solution.py:271
  541.7 107.3 %reduce-scatter.4.cloned.1.call-done = bf16[64,4224]{1,0:T(8,128)(2,1)} async-done(((bf16[1024,4224]{1,0:T(8,128)(2,1)}), bf16[64,4224]{1,0:T(8,128)(2,1)}) %reduce-scatter.4.cloned.1.call-update) | async-done | bytes 540688 | tf_op jit(solution)/shard_map/reduce_scatter | solution.py:271
  (156 shorter events, 81.8 us)
Async XLA Ops:
  7.2 9.1 %copy-start.5 = (bf16[2,1,64,1024]{3,2,1,0:T(8,128)(2,1)S(1)}, bf16[2,1,64,1024]{3,2,1,0:T(8,128)(2,1)}, u32[]{:S(2)}) copy-start(bf16[2,1,64,1024]{3,2,1,0:T(8,128)(2,1)} %param.15) | copy-start | bytes 786436
  7.2 9.5 %copy-start.19 = (s32[2,1]{0,1:T(1,128)S(1)}, s32[2,1]{0,1:T(1,128)}, u32[]{:S(2)}) copy-start(s32[2,1]{0,1:T(1,128)} %param.17) | copy-start | bytes 28
  7.2 86.4 %all-gather.6.cloned.1.call-start = ((), (), s32[]{:S(2)}) async-start(), calls=%async_computation.3 | async-start | bytes 9191424 | tf_op jit(solution)/shard_map/all_gather | solution.py:237
  14.8 153.9 %all-gather.10.cloned.1.call-start = ((), (), s32[]{:S(2)}) async-start(), calls=%async_computation.8 | async-start | bytes 8912896 | tf_op jit(solution)/shard_map/all_gather | solution.py:239
  15.5 228.2 %all-gather.8.cloned.1.call-start = ((), (), s32[]{:S(2)}) async-start(), calls=%async_computation.7 | async-start | bytes 8912896 | tf_op jit(solution)/shard_map/all_gather | solution.py:238
  16.3 416.3 %reduce-scatter.8.cloned.1.call-start = ((), (), s32[]{:S(2)}) async-start(), calls=%async_computation.6 | async-start | bytes 8912896 | tf_op jit(solution)/shard_map/reduce_scatter | solution.py:271
  252.4 9.3 %collective-permute-start = (bf16[2,64,1024]{2,1,0:T(8,128)(2,1)S(1)}, bf16[2,64,1024]{2,1,0:T(8,128)(2,1)S(1)}, u32[]{:S(2)}, u32[]{:S(2)}) collective-permute-start(bf16[2,64,1024]{2,1,0:T(8,128)(2,1)S(1)} %fusion.80), channel_id=1, source_target_pairs={{0,16},{1,17},{2,18},{3,19},{4,20},{5,21},{6,22},{7,23},{8,24},{9,... | collective-permute-start | bytes 786440 | tf_op jit(solution)/shard_map/ppermute | solution.py:18
  267.1 26.4 %copy-start.3 = (bf16[2,64,16,64]{3,2,1,0:T(8,128)(2,1)}, bf16[2,64,16,64]{3,2,1,0:T(8,128)(2,1)S(1)}, u32[]{:S(2)}) copy-start(bf16[2,64,16,64]{3,2,1,0:T(8,128)(2,1)S(1)} %reshape.322) | copy-start | bytes 786436
  268.4 2.6 copy-start.8
  293.5 2.4 copy-start.1
  293.5 2.4 copy-start.4
  296.0 5.2 copy-start.10
  310.9 5.5 copy-start.16
  310.9 5.5 copy-start.18
  316.8 9.6 %collective-permute-start.1 = (bf16[2,64,1024]{2,1,0:T(8,128)(2,1)S(1)}, bf16[2,64,1024]{2,1,0:T(8,128)(2,1)S(1)}, u32[]{:S(2)}, u32[]{:S(2)}) collective-permute-start(bf16[2,64,1024]{2,1,0:T(8,128)(2,1)S(1)} %fusion.125), channel_id=1, source_target_pairs={{16,0},{17,1},{18,2},{19,3},{20,4},{21,5},{22,6},{23,7},{24,8},{25... | collective-permute-start | bytes 786440 | tf_op jit(solution)/shard_map/ppermute | solution.py:18
  326.6 4.7 copy-start.6
  331.3 208.3 %reduce-scatter.6.cloned.1.call-start = ((), (), s32[]{:S(2)}) async-start(), calls=%async_computation.5 | async-start | bytes 8912896 | tf_op jit(solution)/shard_map/reduce_scatter | solution.py:271
  345.1 303.8 %reduce-scatter.4.cloned.1.call-start = ((), (), s32[]{:S(2)}) async-start(), calls=%async_computation.4 | async-start | bytes 9191424 | tf_op jit(solution)/shard_map/reduce_scatter | solution.py:271
  345.4 7.7 %copy-start.7 = (bf16[2,64,1024]{2,1,0:T(8,128)(2,1)S(1)}, bf16[2,64,1024]{2,1,0:T(8,128)(2,1)}, u32[]{:S(2)}) copy-start(bf16[2,64,1024]{2,1,0:T(8,128)(2,1)} %copy-done.6) | copy-start | bytes 786436
  388.7 1.9 copy-start.13
  388.7 1.9 copy-start.14
  388.7 1.9 copy-start.15
  390.6 1.9 copy-start.12
  396.3 5.7 copy-start.17
  (4 other events, 4.6 us)
Sparse Core Ops, SparseCore 0:
  14.9 78.6 all-gather.5
  95.7 72.8 all-gather.9
  170.8 72.8 all-gather.7
  331.4 101.1 reduce-scatter.7
  436.5 103.0 reduce-scatter.5
  543.5 105.4 reduce-scatter.3
